TPU v7x, 32 devices: a whole 2x2x4 slice. The times are simulated.
32 devices in a mesh: replica: 2 (over y), shard: 2 (over x), tensor: 8 (over z, core).
Axes of the slice: x: 2, y: 2, z: 4, core: 2. Of those that a mesh axis runs over, the one named last changes fastest.
Arguments:
- layer_input: bfloat16 [32768, 1024], P(('replica', 'shard', 'tensor')), may hold values from -6 to 6
- segment_ids: int32 [32, 1024], P(('replica', 'shard')), may hold values from 0 to 3, as said below
- qkv_weight: bfloat16 [3, 1024, 1024], P(None, 'shard', 'tensor'), may hold values from -0.1875 to 0.1875
- qkv_bias: float32 [2, 1024], P(None, 'tensor'), may hold values from -1.2 to 1.2
- out_weight: bfloat16 [1024, 1024], P('tensor', 'shard'), may hold values from -1.5 to 1.5
- out_bias: float32 [1024], replicated, may hold values from -3 to 3
- norm1_gain: float32 [1024], replicated, may hold values from 0.5 to 1.5
- norm1_bias: float32 [1024], replicated, may hold values from -3 to 3
- up_weight: bfloat16 [1024, 4096], P('shard', 'tensor'), may hold values from -0.1875 to 0.1875
- up_bias: float32 [4096], P('tensor'), may hold values from -3 to 3
- down_weight: bfloat16 [4096, 1024], P('tensor', 'shard'), may hold values from -0.09375 to 0.09375
- down_bias: float32 [1024], replicated, may hold values from -3 to 3
- norm2_gain: float32 [1024], replicated, may hold values from 0.5 to 1.5
- norm2_bias: float32 [1024], replicated, may hold values from -3 to 3
- output_grad: bfloat16 [32768, 1024], P(('replica', 'shard', 'tensor')), may hold values from -6 to 6
Outputs:
- activations: bfloat16 [32768, 1024], P(('replica', 'shard', 'tensor'))
- input_grad: float32 [32768, 1024], P(('replica', 'shard', 'tensor'))
- qkv_weight_grad: float32 [3, 1024, 1024], P(None, 'shard', 'tensor')
- qkv_bias_grad: float32 [2, 1024], P(None, 'tensor')
- out_weight_grad: float32 [1024, 1024], P('tensor', 'shard')
- out_bias_grad: float32 [1024], replicated
- norm1_gain_grad: float32 [1024], replicated
- norm1_bias_grad: float32 [1024], replicated
- up_weight_grad: float32 [1024, 4096], P('shard', 'tensor')
- up_bias_grad: float32 [4096], P('tensor')
- down_weight_grad: float32 [4096, 1024], P('tensor', 'shard')
- down_bias_grad: float32 [1024], replicated
- norm2_gain_grad: float32 [1024], replicated
- norm2_bias_grad: float32 [1024], replicated
Inputs may be any that keep to these rules, and one draw needn't show every extreme that they name: `segment_ids`: within each sequence the ids never fall and every id from 0 to 3 occurs; each document holds 128 to 512 tokens, and one in each sequence holds exactly 512.
All inputs are finite; a program needn't handle non-finite values.
Results may differ from a plain program's by a relative error of at most 0.02.
Values may be sent and summed in bfloat16 or wider, within the bound.
No kernel may reach another device: no remote copies, remote signals or barrier semaphores. Data moves between devices by JAX's collectives and lax.ppermute only.
A program may use at most 256 MiB of HBM per device.

v0:
```python
import math
import jax
import jax.numpy as jnp
from jax import lax
from jax.sharding import PartitionSpec as P

HEAD_DIM = 64
LEN = 1024
EPSILON = 1e-05
NEG_FILL = -1e30
CONTRACT_ROWS = (((0,), (0,)), ((), ()))
CONTRACT_COLS = (((1,), (1,)), ((), ()))
OWNERS = ("shard", "tensor")
EVERYONE = ("replica", "shard", "tensor")


def gather_blocks(weight):
    blocks = lax.all_gather(weight, OWNERS, axis=0, tiled=False)
    return blocks.reshape((lax.axis_size("shard"), lax.axis_size("tensor")) + weight.shape)


def gather_qkv(weight):
    blocks = gather_blocks(weight)
    return blocks.transpose(2, 0, 3, 1, 4).reshape(3, -1, blocks.shape[1] * blocks.shape[4])


def gather_row_col(weight):
    blocks = gather_blocks(weight)
    return blocks.transpose(0, 2, 1, 3).reshape(-1, blocks.shape[1] * blocks.shape[3])


def gather_col_row(weight):
    blocks = gather_blocks(weight)
    return blocks.transpose(1, 2, 0, 3).reshape(-1, blocks.shape[0] * blocks.shape[3])


def scatter_blocks(blocks):
    flat = blocks.reshape((-1,) + blocks.shape[2:])
    owned = lax.psum_scatter(flat, OWNERS, scatter_dimension=0, tiled=False)
    return lax.psum(owned, "replica").astype(jnp.float32)


def scatter_qkv(grad):
    shards, tensors = (lax.axis_size("shard"), lax.axis_size("tensor"))
    three, rows, cols = grad.shape
    blocks = grad.reshape(three, shards, rows // shards, tensors, cols // tensors)
    return scatter_blocks(blocks.transpose(1, 3, 0, 2, 4))


def scatter_row_col(grad):
    shards, tensors = (lax.axis_size("shard"), lax.axis_size("tensor"))
    rows, cols = grad.shape
    blocks = grad.reshape(shards, rows // shards, tensors, cols // tensors)
    return scatter_blocks(blocks.transpose(0, 2, 1, 3))


def scatter_col_row(grad):
    shards, tensors = (lax.axis_size("shard"), lax.axis_size("tensor"))
    rows, cols = grad.shape
    blocks = grad.reshape(tensors, rows // tensors, shards, cols // shards)
    return scatter_blocks(blocks.transpose(2, 0, 1, 3))


def normalize(residual, gain_vec, shift_vec):
    center = residual - jnp.mean(residual, axis=-1, keepdims=True)
    spread = lax.rsqrt(jnp.mean(center * center, axis=-1, keepdims=True) + EPSILON)
    normed = center * spread
    return (normed * gain_vec + shift_vec, normed, spread)


def norm_back(incoming, normed, spread, gain_vec):
    scaled = incoming * gain_vec
    back_grad = spread * (
        scaled
        - jnp.mean(scaled, axis=-1, keepdims=True)
        - normed * jnp.mean(scaled * normed, axis=-1, keepdims=True)
    )
    return (back_grad, jnp.sum(incoming * normed, axis=0), jnp.sum(incoming, axis=0))


def masked_scores(queries, key_rows, same_doc):
    scores = jnp.einsum(
        "qhd,khd->hqk", queries, key_rows, preferred_element_type=jnp.float32
    ) * HEAD_DIM ** (-0.5)
    return jnp.where(same_doc[None], scores, NEG_FILL)


def attend(queries, key_rows, value_rows, same_doc):
    scores = masked_scores(queries, key_rows, same_doc)
    row_max = jnp.max(scores, axis=-1, keepdims=True)
    raw_weights = jnp.exp(scores - row_max)
    row_total = jnp.sum(raw_weights, axis=-1, keepdims=True)
    attn_probs = raw_weights / row_total
    log_total = row_max + jnp.log(row_total)
    mixed_heads = jnp.einsum(
        "hqk,khd->qhd",
        attn_probs.astype(jnp.bfloat16),
        value_rows,
        preferred_element_type=jnp.float32,
    )
    return (mixed_heads.astype(jnp.bfloat16), log_total)


def attend_back(queries, key_rows, value_rows, same_doc, log_total, mixed_grad):
    scores = masked_scores(queries, key_rows, same_doc)
    attn_probs = jnp.exp(scores - log_total)
    prob_grad = jnp.einsum(
        "qhd,khd->hqk", mixed_grad, value_rows, preferred_element_type=jnp.float32
    )
    value_grad = jnp.einsum(
        "hqk,qhd->khd",
        attn_probs.astype(jnp.bfloat16),
        mixed_grad,
        preferred_element_type=jnp.float32,
    )
    inner_sum = jnp.sum(attn_probs * prob_grad, axis=-1, keepdims=True)
    score_low = (attn_probs * (prob_grad - inner_sum)).astype(jnp.bfloat16)
    query_grad = jnp.einsum(
        "hqk,khd->qhd", score_low, key_rows, preferred_element_type=jnp.float32
    ) * HEAD_DIM ** (-0.5)
    key_grad = jnp.einsum(
        "hqk,qhd->khd", score_low, queries, preferred_element_type=jnp.float32
    ) * HEAD_DIM ** (-0.5)
    return (query_grad, key_grad, value_grad)


def body(
    layer_input,
    segment_ids,
    qkv_weight,
    qkv_bias,
    out_weight,
    out_bias,
    norm1_gain,
    norm1_bias,
    up_weight,
    up_bias,
    down_weight,
    down_bias,
    norm2_gain,
    norm2_bias,
    output_grad,
):
    rows, width = layer_input.shape
    tensor_index = lax.axis_index("tensor")
    tensor_count = lax.axis_size("tensor")
    sharers = max(1, LEN // rows)
    seqs_here = max(1, rows // LEN)
    query_rows = min(rows, LEN)
    sharing = [list(range(i, i + sharers)) for i in range(0, tensor_count, sharers)]
    w_qkv = gather_qkv(qkv_weight)
    bias_qkv = lax.all_gather(qkv_bias, "tensor", axis=1, tiled=True)
    bias_up = lax.all_gather(up_bias, "tensor", axis=0, tiled=True)
    w_out = gather_col_row(out_weight)
    w_up = gather_row_col(up_weight)
    w_down = gather_col_row(down_weight)
    first_seq = tensor_index * rows // LEN
    key_segments = lax.dynamic_slice_in_dim(segment_ids, first_seq, seqs_here, 0)
    query_start = tensor_index * rows % LEN
    query_segments = lax.dynamic_slice_in_dim(key_segments, query_start, query_rows, 1)
    same_doc = query_segments[:, :, None] == key_segments[:, None, :]
    heads = width // HEAD_DIM
    group = 2

    def by_head(rows_array, length):
        split = rows_array.reshape(seqs_here, length, heads // group, group, HEAD_DIM)
        return split.transpose(0, 2, 1, 3, 4)

    def from_heads(blocks):
        return blocks.transpose(0, 2, 1, 3, 4).reshape(-1, width)

    def whole_rows(rows_array):
        if sharers == 1:
            return rows_array
        return lax.all_gather(rows_array, "tensor", axis_index_groups=sharing, axis=0, tiled=True)

    def own_rows(rows_array):
        if sharers == 1:
            return rows_array
        return lax.psum_scatter(
            rows_array, "tensor", axis_index_groups=sharing, scatter_dimension=0, tiled=True
        )

    projected = jnp.einsum("td,jdc->jtc", layer_input, w_qkv, preferred_element_type=jnp.float32)
    queries = (projected[0] + bias_qkv[0]).astype(jnp.bfloat16)
    key_rows = whole_rows(projected[1].astype(jnp.bfloat16))
    value_rows = whole_rows((projected[2] + bias_qkv[1]).astype(jnp.bfloat16))
    queries = by_head(queries, query_rows)
    key_rows = by_head(key_rows, LEN)
    value_rows = by_head(value_rows, LEN)
    mixed, log_total = ([], [])
    for s in range(seqs_here):
        one_mixed, one_log = lax.map(
            lambda item: attend(*item, same_doc[s]), (queries[s], key_rows[s], value_rows[s])
        )
        mixed.append(one_mixed)
        log_total.append(one_log)
    mixed_rows = from_heads(jnp.stack(mixed))
    residual_one = (
        layer_input.astype(jnp.float32)
        + jnp.dot(mixed_rows, w_out, preferred_element_type=jnp.float32)
        + out_bias
    )
    hidden_one, normed_one, spread_one = normalize(residual_one, norm1_gain, norm1_bias)
    hidden_low = hidden_one.astype(jnp.bfloat16)
    pre_act = jnp.dot(hidden_low, w_up, preferred_element_type=jnp.float32) + bias_up
    activ = jax.nn.gelu(pre_act, approximate=False).astype(jnp.bfloat16)
    residual_two = (
        hidden_one + jnp.dot(activ, w_down, preferred_element_type=jnp.float32) + down_bias
    )
    final_out, normed_two, spread_two = normalize(residual_two, norm2_gain, norm2_bias)
    resid_two_grad, gain_two_grad, shift_two_grad = norm_back(
        output_grad.astype(jnp.float32), normed_two, spread_two, norm2_gain
    )
    down_bias_part = jnp.sum(resid_two_grad, axis=0)
    branch_grad = resid_two_grad.astype(jnp.bfloat16)
    down_grad = lax.dot_general(
        activ, branch_grad, CONTRACT_ROWS, preferred_element_type=jnp.float32
    ).astype(jnp.bfloat16)
    down_owned = scatter_col_row(down_grad)
    activ_grad = lax.dot_general(
        branch_grad, w_down, CONTRACT_COLS, preferred_element_type=jnp.float32
    )
    normal_cdf = 0.5 * (1.0 + lax.erf(pre_act * (1.0 / math.sqrt(2.0))))
    normal_pdf = jnp.exp(-0.5 * pre_act * pre_act) * (1.0 / math.sqrt(2.0 * math.pi))
    pre_grad = activ_grad * (normal_cdf + pre_act * normal_pdf)
    up_bias_part = jnp.sum(pre_grad, axis=0)
    pre_low = pre_grad.astype(jnp.bfloat16)
    up_grad = lax.dot_general(
        hidden_low, pre_low, CONTRACT_ROWS, preferred_element_type=jnp.float32
    ).astype(jnp.bfloat16)
    up_owned = scatter_row_col(up_grad)
    back_middle = lax.dot_general(pre_low, w_up, CONTRACT_COLS, preferred_element_type=jnp.float32)
    resid_one_grad, gain_one_grad, shift_one_grad = norm_back(
        resid_two_grad + back_middle, normed_one, spread_one, norm1_gain
    )
    out_bias_part = jnp.sum(resid_one_grad, axis=0)
    attn_grad = resid_one_grad.astype(jnp.bfloat16)
    out_grad = lax.dot_general(
        mixed_rows, attn_grad, CONTRACT_ROWS, preferred_element_type=jnp.float32
    ).astype(jnp.bfloat16)
    out_owned = scatter_col_row(out_grad)
    mixed_grad = lax.dot_general(
        attn_grad, w_out, CONTRACT_COLS, preferred_element_type=jnp.float32
    ).astype(jnp.bfloat16)
    mixed_grad = by_head(mixed_grad, query_rows)
    query_grad, key_grad, value_grad = ([], [], [])
    for s in range(seqs_here):
        grads = lax.map(
            lambda item: attend_back(item[0], item[1], item[2], same_doc[s], item[3], item[4]),
            (queries[s], key_rows[s], value_rows[s], log_total[s], mixed_grad[s]),
        )
        query_grad.append(grads[0])
        key_grad.append(grads[1])
        value_grad.append(grads[2])
    query_grad = from_heads(jnp.stack(query_grad))
    key_grad = own_rows(from_heads(jnp.stack(key_grad)))
    value_grad = own_rows(from_heads(jnp.stack(value_grad)))
    proj_low = [grad.astype(jnp.bfloat16) for grad in (query_grad, key_grad, value_grad)]
    qkv_grad = jnp.stack(
        [
            lax.dot_general(
                layer_input, grad, CONTRACT_ROWS, preferred_element_type=jnp.float32
            ).astype(jnp.bfloat16)
            for grad in proj_low
        ]
    )
    qkv_owned = scatter_qkv(qkv_grad)
    input_grad = resid_one_grad
    for j in range(3):
        input_grad = input_grad + lax.dot_general(
            proj_low[j], w_qkv[j], CONTRACT_COLS, preferred_element_type=jnp.float32
        )
    parts = (
        jnp.sum(query_grad, axis=0),
        jnp.sum(value_grad, axis=0),
        up_bias_part,
        out_bias_part,
        gain_one_grad,
        shift_one_grad,
        down_bias_part,
        gain_two_grad,
        shift_two_grad,
    )
    summed = jnp.sum(lax.all_gather(jnp.concatenate(parts), EVERYONE, axis=0, tiled=False), axis=0)
    ends = [0]
    for part in parts:
        ends.append(ends[-1] + part.shape[0])
    summed = [summed[ends[i] : ends[i + 1]] for i in range(len(parts))]
    width_here = qkv_bias.shape[1]
    hidden_here = up_bias.shape[0]
    qkv_bias_grad = lax.dynamic_slice_in_dim(
        jnp.stack(summed[:2]), tensor_index * width_here, width_here, 1
    )
    up_bias_grad = lax.dynamic_slice_in_dim(summed[2], tensor_index * hidden_here, hidden_here, 0)
    return (
        final_out.astype(jnp.bfloat16),
        input_grad,
        qkv_owned,
        qkv_bias_grad,
        out_owned,
        summed[3],
        summed[4],
        summed[5],
        up_owned,
        up_bias_grad,
        down_owned,
        summed[6],
        summed[7],
        summed[8],
    )


def solution(mesh):
    placed = (
        P(("replica", "shard", "tensor"), None),
        P(("replica", "shard"), None),
        P(None, "shard", "tensor"),
        P(None, "tensor"),
        P("tensor", "shard"),
        P(),
        P(),
        P(),
        P("shard", "tensor"),
        P("tensor"),
        P("tensor", "shard"),
        P(),
        P(),
        P(),
        P(("replica", "shard", "tensor"), None),
    )
    return jax.shard_map(
        body,
        mesh=mesh,
        in_specs=placed,
        out_specs=(
            P(("replica", "shard", "tensor"), None),
            P(("replica", "shard", "tensor"), None),
            P(None, "shard", "tensor"),
            P(None, "tensor"),
            P("tensor", "shard"),
            P(),
            P(),
            P(),
            P("shard", "tensor"),
            P("tensor"),
            P("tensor", "shard"),
            P(),
            P(),
            P(),
        ),
        check_vma=False,
    )
```

profile of v0, /device:TPU:0, one launch (start us, length us, event | category | flops | bytes accessed | tf_op | source)
XLA Modules:
  0.0 1084.6 jit_solution(9665924579139208757)
XLA Ops:
  10.1 13.7 %all_gather.38 = f32[2,1024]{1,0:T(2,128)S(1)} all-gather(f32[2,128]{1,0:T(2,128)} %param.22), channel_id=1, replica_groups=mesh['replica'=2,'shard'=2,'tensor'=8] {'tensor'}, dimensions={1}, use_global_device_ids=true | all-gather | bytes 9216 | tf_op jit(solution)/shard_map/all_gather | solution.py:152
  24.0 3.9 copy.93
  28.0 12.8 %all-gather.5 = f32[8,1,512]{2,1,0:T(1,128)S(1)} all-gather(f32[1,1,512]{2,1,0:T(1,128)S(1)} %bitcast.312), channel_id=1, replica_groups=mesh['replica'=2,'shard'=2,'tensor'=8] {'tensor'}, dimensions={0}, use_global_device_ids=true | all-gather | bytes 18432 | tf_op jit(solution)/shard_map/all_gather | solution.py:153
  43.3 11.1 %all-gather.14.cloned.1.call-done = bf16[2048,512]{1,0:T(8,128)(2,1)} async-done(((bf16[128,512]{1,0:T(8,128)(2,1)}), bf16[2048,512]{1,0:T(8,128)(2,1)}) %all-gather.14.cloned.1.call-update) | async-done | bytes 2097168 | tf_op jit(solution)/shard_map/all_gather | solution.py:18
  54.4 4.3 copy.95
  58.8 58.2 %all-gather.12.cloned.1.call-done = bf16[48,512,128]{2,1,0:T(8,128)(2,1)} async-done(((bf16[3,512,128]{2,1,0:T(8,128)(2,1)}), bf16[48,512,128]{2,1,0:T(8,128)(2,1)}) %all-gather.12.cloned.1.call-update) | async-done | bytes 6291472 | tf_op jit(solution)/shard_map/all_gather | solution.py:18
  116.9 16.2 %copy.94 = bf16[2,8,3,512,128]{3,0,4,1,2:T(2,128)(2,1)} copy(bf16[2,8,3,512,128]{4,3,2,1,0:T(8,128)(2,1)} %bitcast.294) | data formatting | bytes 12582912 | tf_op jit(solution)/shard_map/reshape | solution.py:19
  133.1 11.0 %reshape.287 = bf16[3,1024,1024]{1,2,0:T(8,128)(2,1)} reshape(bf16[3,2,512,8,128]{2,1,4,3,0:T(2,128)(2,1)} %bitcast.265) | data formatting | bytes 12582912 | tf_op jit(solution)/shard_map/reshape | solution.py:24
  144.1 9.7 convolution_bitcast_fusion
  153.8 4.5 copy-done.13
  165.1 84.4 %while.28 = (s32[]{:T(128)}, bf16[8,1024,2,64]{1,3,2,0:T(8,128)(2,1)}, f32[8,2,1024,1]{2,1,3,0:T(2,128)}, bf16[8,1024,2,64]{1,3,2,0:T(8,128)(2,1)}, bf16[8,1024,...) while((s32[]{:T(128)}, ...), condition=%wide.region_3.4_spmd.clone, body=%wide.region_0.3_spmd.clone.sunk | while | flops 563214336 | bytes 30480980 | solution.py:193
  171.2 4.4 fusion.167
  181.8 4.4 fusion.167
  192.3 4.4 fusion.167
  202.8 4.4 fusion.167
  213.3 4.4 fusion.167
  223.9 4.4 fusion.167
  234.4 4.4 fusion.167
  244.9 4.4 fusion.167
  249.5 6.3 fusion.116
  258.6 11.5 %copy.96 = bf16[2,8,512,512]{3,1,2,0:T(8,128)(2,1)} copy(bf16[2,8,512,512]{3,2,1,0:T(8,128)(2,1)} %bitcast.279) | data formatting | bytes 16777216 | tf_op jit(solution)/shard_map/reshape | solution.py:19
  270.1 12.6 %copy.120 = bf16[128,8,8,512]{3,1,2,0:T(8,128)(2,1)} copy(bf16[128,8,8,512]{3,2,1,0:T(8,128)(2,1)} %bitcast.269) | data formatting | bytes 16777216
  282.7 14.9 %copy.97 = bf16[2,8,512,512]{2,1,3,0:T(8,128)(2,1)} copy(bf16[2,8,512,512]{3,2,1,0:T(8,128)(2,1)} %bitcast.280) | data formatting | bytes 16777216 | tf_op jit(solution)/shard_map/reshape | solution.py:19
  297.6 12.2 %copy.121 = bf16[128,8,8,512]{3,1,2,0:T(8,128)(2,1)} copy(bf16[128,8,8,512]{3,2,1,0:T(8,128)(2,1)} %bitcast.270) | data formatting | bytes 16777216
  309.9 47.6 %fusion.60 = (bf16[1024,4096]{1,0:T(8,128)(2,1)}, f32[1024,4096]{1,0:T(8,128)}) fusion(f32[4096]{0:T(1024)S(1)} %bitcast.310, bf16[1024,4096]{1,0:T(8,128)(2,1)} %bitcast.281, bf16[1024,1024]{0,1:T(8,128)(2,1)S(1)} %fusion.108.clone.4), kind=kOutput, calls=%fused_computation.67 | convolution fusion | flops 8866758656 | bytes 35667968 | tf_op jit(solution)/shard_map/dot_general | solution.py:206
  357.6 11.6 %fusion.117 = (f32[1024]{0:T(1024)S(1)}, f32[1024,1024]{0,1:T(8,128)S(1)}) fusion(f32[1024]{0:T(1024)S(1)} %copy-done.54, bf16[1024,4096]{1,0:T(8,128)(2,1)} %get-tuple-element.278, bf16[4096,1024]{0,1:T(8,128)(2,1)S(1)} %bitcast.286, f32[1024]{0:T(1024)S(1)} %copy-done.47, f32[1024]{0:T(1024)S(1)} %copy-done.36, f32[1024]{0:T(1024)S(1)} %copy-done.31, ...), kind=kOutput, calls=%fused_computation.176 | convolution fusion | flops 8597273600 | bytes 25190400 | tf_op jit(solution)/shard_map/dot_general | solution.py:209
  373.4 23.7 %fusion.118 = (f32[4096]{0:T(1024)}, bf16[1024,4096]{1,0:T(8,128)(2,1)}) fusion(f32[1024,4096]{1,0:T(8,128)} %get-tuple-element.279, f32[4096]{0:T(1024)S(1)} %bitcast.311, bf16[4096,1024]{0,1:T(8,128)(2,1)} %bitcast.285, f32[1024]{0:T(1024)S(1)} %broadcast_multiply_fusion.2, f32[1024,1024]{0,1:T(8,128)S(1)} %get-tuple-element.281, ...), kind=kOutput, calls=%fused_computation.177 | convolution fusion | flops 8649699328 | bytes 39899136 | tf_op jit(solution)/shard_map/dot_general | solution.py:221
  397.1 15.3 %multiply_reduce_fusion.1 = (f32[1024]{0:T(1024)}, f32[1024]{0:T(1024)S(1)}, f32[1024]{0:T(1024)S(1)}, f32[1024]{0:T(1024)}, f32[1024,1024]{0,1:T(8,128)}) fusion(f32[1024,1024]{0,1:T(8,128)S(1)} %copy-done.3, f32[1024]{0:T(1024)S(1)} %copy-done.31, f32[1024]{0:T(1024)S(1)} %copy-done.25, f32[1024]{0:T(1024)S(1)} %copy-done.36, ...), kind=kOutput, calls=%fused_computation.108 | convolution fusion | flops 8608804864 | bytes 31506432 | tf_op jit(solution)/shard_map/dot_general | solution.py:233
  412.5 4.4 fusion.112
  419.3 5.3 convolution_convert_fusion.2
  424.6 154.8 %while.29 = (s32[]{:T(128)}, f32[8,1024,2,64]{1,3,2,0:T(8,128)}, bf16[8,1024,2,64]{1,3,2,0:T(8,128)(2,1)}, f32[8,1024,2,64]{1,3,2,0:T(8,128)}, bf16[8,1024,2,64]...) while((s32[]{:T(128)}, f32[8,1024,2,64]{1,3,2,0:T(8,128)}, ...), condition=%wide.region_14.15_spmd.clone, body=%wide.region_12.14_spmd.clone.sunk | while | flops 1374943232 | bytes 70583408 | solution.py:249
  428.5 3.9 multiply_reduce_fusion.7
  447.8 3.9 multiply_reduce_fusion.7
  467.1 3.9 multiply_reduce_fusion.7
  486.5 3.9 multiply_reduce_fusion.7
  505.8 3.9 multiply_reduce_fusion.7
  525.1 3.9 multiply_reduce_fusion.7
  544.4 3.9 multiply_reduce_fusion.7
  563.8 3.9 multiply_reduce_fusion.7
  582.3 3.7 convert_bitcast_fusion.2
  588.5 5.1 reshape.297
  597.0 5.2 convert_bitcast_fusion
  605.6 4.5 stack.36
  610.1 6.0 convert_bitcast_fusion.1
  616.1 4.5 stack.35
  620.6 12.8 %maximum_bitcast_fusion = bf16[2,8,3,512,128]{3,0,4,1,2:T(2,128)(2,1)} fusion(bf16[1,2,512,8,128]{2,1,4,3,0:T(2,128)(2,1)} %stack.36, bf16[1,2,512,8,128]{2,1,4,3,0:T(2,128)(2,1)} %stack.35, bf16[1,2,512,8,128]{2,1,4,3,0:T(2,128)(2,1)S(1)} %stack.34), kind=kLoop, calls=%fused_computation.91 | loop fusion | flops 6291456 | bytes 12582912 | tf_op jit(solution)/shard_map/transpose | solution.py:47
  633.4 16.2 %copy.104 = bf16[2,8,3,512,128]{4,3,2,1,0:T(8,128)(2,1)} copy(bf16[2,8,3,512,128]{3,0,4,1,2:T(2,128)(2,1)} %maximum_bitcast_fusion) | data formatting | bytes 12582912 | tf_op jit(solution)/shard_map/transpose | solution.py:47
  651.3 16.7 %convolution_convert_fusion = bf16[4096,1024]{1,0:T(8,128)(2,1)} fusion(bf16[1024,4096]{1,0:T(8,128)(2,1)} %get-tuple-element.278, bf16[1024,1024]{0,1:T(8,128)(2,1)S(1)} %copy-done.8, f32[1024,1024]{0,1:T(8,128)} %copy-done.4, f32[1024]{0:T(1024)S(1)} %copy-done.39, f32[1024]{0:T(1024)S(1)} %copy-done.41, f32[1024]{0:T(1024)S(1)} %copy-done.45, ...), kind=kOutput, calls=%fused_computation.89 | convolution fusion | flops 8603566080 | bytes 23089152 | tf_op jit(solution)/shard_map/dot_general | solution.py:217
  668.0 14.9 %reshape.301 = bf16[8,512,2,512]{3,2,1,0:T(2,128)(2,1)} reshape(bf16[4096,1024]{1,0:T(8,128)(2,1)} %convolution_convert_fusion) | data formatting | bytes 16777216 | tf_op jit(solution)/shard_map/reshape | solution.py:60
  682.9 8.7 copy.107
  692.3 15.5 %convolution_convert_fusion.1 = bf16[1024,4096]{1,0:T(8,128)(2,1)} fusion(bf16[1024,4096]{1,0:T(8,128)(2,1)} %get-tuple-element.284, f32[1024,1024]{0,1:T(8,128)} %copy-done.2, f32[1024]{0:T(1024)S(1)} %copy-done.48, f32[1024]{0:T(1024)S(1)} %copy-done.37, f32[1024]{0:T(1024)S(1)} %copy-done.32, f32[1024]{0:T(1024)S(1)} %copy-done.26), kind=kOutput, calls=%fused_computation.90 | convolution fusion | flops 8599371776 | bytes 20987904 | tf_op jit(solution)/shard_map/dot_general | solution.py:229
  707.8 12.2 %copy.125 = bf16[128,8,8,512]{3,2,1,0:T(8,128)(2,1)} copy(bf16[128,8,8,512]{3,1,2,0:T(8,128)(2,1)} %bitcast.287) | data formatting | bytes 16777216
  720.0 7.2 bitcast_bitcast_fusion
  727.3 9.9 copy.106
  742.5 5.3 fusion.79
  748.5 6.3 fusion.114
  757.9 4.5 fusion.119
  762.4 89.7 %reduce-scatter.11.cloned.1.call-done = bf16[1,512,512]{2,1,0:T(8,128)(2,1)} async-done(((bf16[16,512,512]{2,1,0:T(8,128)(2,1)}), bf16[1,512,512]{2,1,0:T(8,128)(2,1)}) %reduce-scatter.11.cloned.1.call-update) | async-done | bytes 524304 | tf_op jit(solution)/shard_map/reduce_scatter | solution.py:39
  852.1 107.2 %reduce-scatter.9.cloned.1.call-done = bf16[1,512,512]{2,1,0:T(8,128)(2,1)} async-done(((bf16[16,512,512]{2,1,0:T(8,128)(2,1)}), bf16[1,512,512]{2,1,0:T(8,128)(2,1)}) %reduce-scatter.9.cloned.1.call-update) | async-done | bytes 524304 | tf_op jit(solution)/shard_map/reduce_scatter | solution.py:39
  959.4 4.8 fusion.120
  964.7 5.0 add_add_fusion
  969.7 5.5 copy.109
  977.7 39.8 %all-gather.20.cloned.1.call-done = f32[393216]{0:T(1024)} async-done(((f32[12288]{0:T(1024)}), f32[393216]{0:T(1024)}) %all-gather.20.cloned.1.call-update) | async-done | bytes 1572880 | tf_op jit(solution)/shard_map/all_gather | solution.py:285
  1021.3 49.2 %all-reduce.3.cloned.1.call-done = (bf16[3,512,128]{2,1,0:T(8,128)(2,1)}, bf16[128,512]{1,0:T(8,128)(2,1)}, bf16[512,512]{1,0:T(8,128)(2,1)}, bf16[512,512]{1,0:T(8,128)(2,1)}) async-done(((bf16[3,512,128]{2,1,0:T(8,128)(2,1)}, bf16[128,512]{1,0:T(8,128)(2,1)}, bf16[512,512]{1,0:T(8,128)(2,1)}, bf16[512,512]{1,0:T(8,128)(2,1)}), (bf16[3,512,128]{2,1,0:T(8,128)(2,1)}, bf16[128,512]{1,0:T(8,128)(2,1)}, ...) | async-done | bytes 1572880 | tf_op jit(solution)/shard_map/psum | solution.py:40
  (283 shorter events, 230.4 us)
Async XLA Ops:
  7.2 36.1 %copy-start = (s32[8,1024]{1,0:T(8,128)S(1)}, s32[8,1024]{1,0:T(8,128)}, u32[]{:S(2)}) copy-start(s32[8,1024]{1,0:T(8,128)} %param.20) | copy-start | bytes 98308
  7.2 20.8 %copy-start.52 = (f32[512]{0:T(512)S(1)}, f32[512]{0:T(512)}, u32[]{:S(2)}) copy-start(f32[512]{0:T(512)} %param.28) | copy-start | bytes 6148
  7.2 33.5 %copy-start.18 = (bf16[1024,1024]{1,0:T(8,128)(2,1)S(1)}, bf16[1024,1024]{1,0:T(8,128)(2,1)}, u32[]{:S(2)}) copy-start(bf16[1024,1024]{1,0:T(8,128)(2,1)} %param.33) | copy-start | bytes 6291460
  7.2 47.2 %all-gather.14.cloned.1.call-start = ((), (), s32[]{:S(2)}) async-start(), calls=%async_computation.9 | async-start | bytes 2228224 | tf_op jit(solution)/shard_map/all_gather | solution.py:18
  8.0 109.0 %all-gather.12.cloned.1.call-start = ((), (), s32[]{:S(2)}) async-start(), calls=%async_computation.8 | async-start | bytes 6684672 | tf_op jit(solution)/shard_map/all_gather | solution.py:18
  8.7 249.9 %all-gather.16.cloned.1.call-start = ((), (), s32[]{:S(2)}) async-start(), calls=%async_computation.10 | async-start | bytes 8912896 | tf_op jit(solution)/shard_map/all_gather | solution.py:18
  9.4 273.3 %all-gather.18.cloned.1.call-start = ((), (), s32[]{:S(2)}) async-start(), calls=%async_computation.11 | async-start | bytes 8912896 | tf_op jit(solution)/shard_map/all_gather | solution.py:18
  10.0 752.4 %reduce-scatter.7.cloned.1.call-start = ((), (), s32[]{:S(2)}) async-start(), calls=%async_computation.5 | async-start | bytes 2228224 | tf_op jit(solution)/shard_map/reduce_scatter | solution.py:39
  153.8 4.5 copy-start.13
  165.1 84.4 %copy-start.53 = (f32[1024]{0:T(1024)S(1)}, f32[1024]{0:T(1024)}, u32[]{:S(2)}) copy-start(f32[1024]{0:T(1024)} %param.24) | copy-start | bytes 12292
  249.5 6.4 copy-start.11
  249.5 6.4 copy-start.21
  255.9 2.0 copy-start.2
  255.9 2.0 copy-start.35
  255.9 2.0 copy-start.46
  255.9 2.6 copy-start.24
  257.9 12.2 %copy-start.30 = (f32[1024]{0:T(1024)}, f32[1024]{0:T(1024)S(1)}, u32[]{:S(2)}) copy-start(f32[1024]{0:T(1024)S(1)} %add_rsqrt_fusion.1) | copy-start | bytes 12292
  309.8 47.7 %copy-start.3 = (f32[1024,1024]{0,1:T(8,128)S(1)}, f32[1024,1024]{0,1:T(8,128)}, u32[]{:S(2)}) copy-start(f32[1024,1024]{0,1:T(8,128)} %copy-done.2) | copy-start | bytes 12582916
  309.8 47.7 %copy-start.14 = (bf16[128,8,8,512]{3,1,2,0:T(8,128)(2,1)S(1)}, bf16[128,8,8,512]{3,1,2,0:T(8,128)(2,1)}, u32[]{:S(2)}) copy-start(bf16[128,8,8,512]{3,1,2,0:T(8,128)(2,1)} %copy.121) | copy-start | bytes 25165828
  309.8 47.7 %copy-start.25 = (f32[1024]{0:T(1024)S(1)}, f32[1024]{0:T(1024)}, u32[]{:S(2)}) copy-start(f32[1024]{0:T(1024)} %copy-done.24) | copy-start | bytes 12292
  309.8 47.7 %copy-start.31 = (f32[1024]{0:T(1024)S(1)}, f32[1024]{0:T(1024)}, u32[]{:S(2)}) copy-start(f32[1024]{0:T(1024)} %copy-done.30) | copy-start | bytes 12292
  309.8 47.7 %copy-start.36 = (f32[1024]{0:T(1024)S(1)}, f32[1024]{0:T(1024)}, u32[]{:S(2)}) copy-start(f32[1024]{0:T(1024)} %param.25) | copy-start | bytes 12292
  309.8 47.7 %copy-start.47 = (f32[1024]{0:T(1024)S(1)}, f32[1024]{0:T(1024)}, u32[]{:S(2)}) copy-start(f32[1024]{0:T(1024)} %param.26) | copy-start | bytes 12292
  309.9 47.7 %copy-start.54 = (f32[1024]{0:T(1024)S(1)}, f32[1024]{0:T(1024)}, u32[]{:S(2)}) copy-start(f32[1024]{0:T(1024)} %param.30) | copy-start | bytes 12292
  369.2 27.9 %copy-start.4 = (f32[1024,1024]{0,1:T(8,128)}, f32[1024,1024]{0,1:T(8,128)S(1)}, u32[]{:S(2)}) copy-start(f32[1024,1024]{0,1:T(8,128)S(1)} %get-tuple-element.281) | copy-start | bytes 12582916
  369.2 3.1 copy-start.7
  369.2 3.1 copy-start.44
  369.2 27.8 %copy-start.27 = (f32[1024]{0:T(1024)}, f32[1024]{0:T(1024)S(1)}, u32[]{:S(2)}) copy-start(f32[1024]{0:T(1024)S(1)} %broadcast_multiply_fusion.4) | copy-start | bytes 12292
  372.3 24.8 %copy-start.33 = (f32[1024]{0:T(1024)}, f32[1024]{0:T(1024)S(1)}, u32[]{:S(2)}) copy-start(f32[1024]{0:T(1024)S(1)} %add_rsqrt_fusion) | copy-start | bytes 12292
  372.3 24.8 %slice-start = ((s8[8388608]{0:T(1024)(128)(4,1)}), s8[4194304]{0:T(1024)(128)(4,1)S(1)}, s32[]{:S(2)}) async-start(s8[8388608]{0:T(1024)(128)(4,1)} %bitcast.282), calls=%async_computation.14 | async-start | bytes 8388608
  373.3 23.7 %copy-start.38 = (f32[1024]{0:T(1024)}, f32[1024]{0:T(1024)S(1)}, u32[]{:S(2)}) copy-start(f32[1024]{0:T(1024)S(1)} %broadcast_multiply_fusion.2) | copy-start | bytes 12292
  373.4 23.7 %copy-start.40 = (f32[1024]{0:T(1024)}, f32[1024]{0:T(1024)S(1)}, u32[]{:S(2)}) copy-start(f32[1024]{0:T(1024)S(1)} %broadcast_multiply_fusion.3) | copy-start | bytes 12292
  373.4 23.7 %slice-start.1 = ((s8[8388608]{0:T(1024)(128)(4,1)}), s8[4194304]{0:T(1024)(128)(4,1)S(1)}, s32[]{:S(2)}) async-start(s8[8388608]{0:T(1024)(128)(4,1)} %bitcast.282), calls=%async_computation.15 | async-start | bytes 8388608
  412.5 4.4 copy-start.20
  416.8 2.4 copy-start.5
  419.3 5.3 copy-start.22
  579.4 2.9 copy-start.19
  582.1 3.9 copy-start.16
  588.5 8.5 copy-start.9
  597.0 165.4 %reduce-scatter.5.cloned.1.call-start = ((), (), s32[]{:S(2)}) async-start(), calls=%async_computation.4 | async-start | bytes 6684672 | tf_op jit(solution)/shard_map/reduce_scatter | solution.py:39
  649.7 1.6 copy-start.8
  649.7 1.6 copy-start.28
  649.7 1.6 copy-start.34
  649.7 1.6 copy-start.39
  649.7 1.6 copy-start.41
  649.7 1.6 copy-start.45
  649.7 202.4 %reduce-scatter.11.cloned.1.call-start = ((), (), s32[]{:S(2)}) async-start(), calls=%async_computation.7 | async-start | bytes 8912896 | tf_op jit(solution)/shard_map/reduce_scatter | solution.py:39
  691.6 0.7 copy-start.37
  691.6 0.7 copy-start.48
  691.6 267.7 %reduce-scatter.9.cloned.1.call-start = ((), (), s32[]{:S(2)}) async-start(), calls=%async_computation.6 | async-start | bytes 8912896 | tf_op jit(solution)/shard_map/reduce_scatter | solution.py:39
  737.2 5.3 copy-start.43
  737.2 5.3 copy-start.42
  737.2 5.3 copy-start.51
  737.2 5.3 copy-start.50
  737.2 5.3 copy-start.49
  737.2 280.3 %all-gather.20.cloned.1.call-start = ((), (), s32[]{:S(2)}) async-start(), calls=%async_computation.12 | async-start | bytes 1622016 | tf_op jit(solution)/shard_map/all_gather | solution.py:285
  748.5 321.9 %all-reduce.3.cloned.1.call-start = ((), (), s32[]{:S(2)}) async-start(), calls=%async_computation.13 | async-start | bytes 3145728 | tf_op jit(solution)/shard_map/psum | solution.py:40
  755.4 2.5 copy-start.17
  959.3 4.9 copy-start.6
  959.3 4.9 copy-start.10
  959.3 5.3 copy-start.12
  969.7 5.5 copy-start.15
  975.2 102.2 %copy-start.1 = (s32[8,1024]{1,0:T(8,128)S(1)}, s32[8,1024]{1,0:T(8,128)}, u32[]{:S(2)}) copy-start(s32[8,1024]{1,0:T(8,128)} %param.20) | copy-start | bytes 98308
  1070.4 6.3 copy-start.23
  (3 other events, 2.0 us)
Sparse Core Ops, SparseCore 0:
  10.2 44.1 all-gather.13
  56.8 60.1 all-gather.11
  119.1 72.9 all-gather.15
  194.2 72.9 all-gather.17
  597.1 60.4 reduce-scatter.6
  661.3 84.0 reduce-scatter.4
  749.5 102.5 reduce-scatter.10
  856.2 103.0 reduce-scatter.8
  962.9 54.6 all-gather.19
  1019.9 50.4 all-reduce.2
where the time goes:
time: 1100 us; the launch traced here: 1080 us
  matrix products  363 us (33%)
  waiting for transfers between devices  358 us (33%)
  local copies, waits for them, and re-layouts  222 us (20%)
  other arithmetic  98.6 us (9%)
  blocking collectives  26.5 us (2%)
  between operations  15.4 us (1%)
    reduce_scatter x4, waiting for transfers between devices, scatter_blocks(): owned = lax.psum_scatter(flat, OWNERS, scatter_dimension=0, tiled=False)  197 us
    all_gather x4, waiting for transfers between devices, gather_blocks(): blocks = lax.all_gather(weight, OWNERS, axis=0, tiled=False)  69.3 us
    unnamed x132, local copies, waits for them, and re-layouts  66.8 us
    psum x1, waiting for transfers between devices, scatter_blocks(): return lax.psum(owned, 'replica').astype(jnp.float32)  49.2 us
    dot_general x1, matrix products, body(): jnp.dot(hidden_low, w_up, preferred_element_type=jnp.float32) + bias_up  47.6 us
    reshape x4, local copies, waits for them, and re-layouts, gather_blocks(): blocks.reshape((lax.axis_size('shard'), lax.axis_size('tensor')) + weight...  46.9 us
    dot_general x16, matrix products, masked_scores(): jnp.einsum('qhd,khd->hqk', queries, key_rows, preferred_element_type=jnp....  41.3 us
    all_gather x1, waiting for transfers between devices, body(): lax.all_gather(jnp.concatenate(parts), EVERYONE, axis=0, tiled=False)  39.8 us
  transfers between devices with their start and end apart: 10, of which 6 were waited for; matrix products, arithmetic and copies ran while one was open for 33% of the time, Pallas kernels for 0%

commit v1 on v0

--- a/solution.py
+++ b/solution.py
@@ -1,8 +1,10 @@
+import functools
 import math
 import jax
 import jax.numpy as jnp
 from jax import lax
 from jax.sharding import PartitionSpec as P
+from jax.lax import all_gather
 
 HEAD_DIM = 64
 LEN = 1024
@@ -14,6 +16,14 @@
 EVERYONE = ("replica", "shard", "tensor")
 
 
+def order_fields(vec, group_axis):
+    carry = all_gather(vec, group_axis)
+    return jnp.sum(carry, axis=0)
+
+
+load_the_edge = functools.partial(order_fields, group_axis="replica")
+
+
 def gather_blocks(weight):
     blocks = lax.all_gather(weight, OWNERS, axis=0, tiled=False)
     return blocks.reshape((lax.axis_size("shard"), lax.axis_size("tensor")) + weight.shape)
@@ -37,7 +47,7 @@
 def scatter_blocks(blocks):
     flat = blocks.reshape((-1,) + blocks.shape[2:])
     owned = lax.psum_scatter(flat, OWNERS, scatter_dimension=0, tiled=False)
-    return lax.psum(owned, "replica").astype(jnp.float32)
+    return load_the_edge(owned).astype(jnp.float32)
 
 
 def scatter_qkv(grad):

time: 1100 us -> 941 us (0.86)
  waiting for transfers between devices: 358 us -> 187 us
  blocking collectives: 26.5 us -> 46.4 us
  matrix products: 363 us -> 375 us
    reduce_scatter x4, waiting for transfers between devices: 197 us -> 87.6 us  [scatter_blocks(): owned = lax.psum_scatter(flat, OWNERS, scatter_dimension=0, tiled=False)]
    psum x1 -> x0, waiting for transfers between devices: 49.2 us -> none  [scatter_blocks(): return lax.psum(owned, 'replica').astype(jnp.float32)]
    transpose x5 -> x0, local copies, waits for them, and re-layouts: 45.3 us -> none  [the longest x2 17.1 us: scatter_row_col(): return scatter_blocks(blocks.transpose(0, 2, 1, 3))]
    all_gather x1, waiting for transfers between devices: 39.8 us -> 0.01 us  [body(): lax.all_gather(jnp.concatenate(parts), EVERYONE, axis=0, tiled=False)]
    all_gather x0 -> x2, waiting for transfers between devices: none -> 26.9 us  [order_fields(): carry = all_gather(vec, group_axis)]
    all_gather x0 -> x2, blocking collectives: none -> 19.9 us  [order_fields(): carry = all_gather(vec, group_axis)]
    another operation x3 -> x6, local copies, waits for them, and re-layouts: 12.4 us -> 28.5 us  [body(): jnp.stack([lax.dot_general(layer_input, grad, CONTRACT_ROWS, preferred_el...]
    transpose x1 -> x0, other arithmetic: 12.8 us -> none  [scatter_qkv(): return scatter_blocks(blocks.transpose(1, 3, 0, 2, 4))]
  transfers between devices with their start and end apart: 10 -> 11, of which waited for: 6 -> 6; matrix products, arithmetic and copies ran while one was open for 33% -> 58% of each run, Pallas kernels for 0% -> 0%
where the time goes in v1:
time: 941 us; the launch traced here: 927 us
  matrix products  375 us (40%)
  local copies, waits for them, and re-layouts  213 us (23%)
  waiting for transfers between devices  187 us (20%)
  other arithmetic  90.1 us (10%)
  blocking collectives  46.4 us (5%)
  between operations  15 us (2%)
    reduce_scatter x4, waiting for transfers between devices, scatter_blocks(): owned = lax.psum_scatter(flat, OWNERS, scatter_dimension=0, tiled=False)  87.6 us
    unnamed x94, local copies, waits for them, and re-layouts  70.1 us
    all_gather x4, waiting for transfers between devices, gather_blocks(): blocks = lax.all_gather(weight, OWNERS, axis=0, tiled=False)  69.5 us
    dot_general x1, matrix products, body(): jnp.dot(hidden_low, w_up, preferred_element_type=jnp.float32) + bias_up  47.8 us
    reshape x4, local copies, waits for them, and re-layouts, gather_blocks(): blocks.reshape((lax.axis_size('shard'), lax.axis_size('tensor')) + weight...  46.8 us
    dot_general x16, matrix products, masked_scores(): jnp.einsum('qhd,khd->hqk', queries, key_rows, preferred_element_type=jnp....  41.4 us
    dot_general x8, matrix products, attend(): jnp.einsum('hqk,khd->qhd', attn_probs.astype(jnp.bfloat16), value_rows, p...  35.2 us
    dot_general x8, matrix products, attend_back(): jnp.einsum('hqk,qhd->khd', attn_probs.astype(jnp.bfloat16), mixed_grad, p...  34.2 us
  transfers between devices with their start and end apart: 11, of which 6 were waited for; matrix products, arithmetic and copies ran while one was open for 58% of the time, Pallas kernels for 0%

profile of v1, /device:TPU:0, one launch (start us, length us, event | category | flops | bytes accessed | tf_op | source)
XLA Modules:
  0.0 927.4 jit_solution(11224028913519090012)
XLA Ops:
  10.1 13.7 %all_gather.50 = f32[2,1024]{1,0:T(2,128)S(1)} all-gather(f32[2,128]{1,0:T(2,128)} %param.22), channel_id=1, replica_groups=mesh['replica'=2,'shard'=2,'tensor'=8] {'tensor'}, dimensions={1}, use_global_device_ids=true | all-gather | bytes 9216 | tf_op jit(solution)/shard_map/all_gather | solution.py:162
  28.0 12.8 %all-gather.5 = f32[8,1,512]{2,1,0:T(1,128)S(1)} all-gather(f32[1,1,512]{2,1,0:T(1,128)S(1)} %bitcast.300), channel_id=1, replica_groups=mesh['replica'=2,'shard'=2,'tensor'=8] {'tensor'}, dimensions={0}, use_global_device_ids=true | all-gather | bytes 18432 | tf_op jit(solution)/shard_map/all_gather | solution.py:163
  43.3 11.3 %all-gather.20.cloned.1.call-done = bf16[2048,512]{1,0:T(8,128)(2,1)} async-done(((bf16[128,512]{1,0:T(8,128)(2,1)}), bf16[2048,512]{1,0:T(8,128)(2,1)}) %all-gather.20.cloned.1.call-update) | async-done | bytes 2097168 | tf_op jit(solution)/shard_map/all_gather | solution.py:28
  54.5 4.3 copy.95
  58.8 58.2 %all-gather.18.cloned.1.call-done = bf16[48,512,128]{2,1,0:T(8,128)(2,1)} async-done(((bf16[3,512,128]{2,1,0:T(8,128)(2,1)}), bf16[48,512,128]{2,1,0:T(8,128)(2,1)}) %all-gather.18.cloned.1.call-update) | async-done | bytes 6291472 | tf_op jit(solution)/shard_map/all_gather | solution.py:28
  117.0 16.2 %copy.94 = bf16[2,8,3,512,128]{3,0,4,1,2:T(2,128)(2,1)} copy(bf16[2,8,3,512,128]{4,3,2,1,0:T(8,128)(2,1)} %bitcast.286) | data formatting | bytes 12582912 | tf_op jit(solution)/shard_map/reshape | solution.py:29
  133.2 11.0 %reshape.287 = bf16[3,1024,1024]{1,2,0:T(8,128)(2,1)} reshape(bf16[3,2,512,8,128]{2,1,4,3,0:T(2,128)(2,1)} %bitcast.261) | data formatting | bytes 12582912 | tf_op jit(solution)/shard_map/reshape | solution.py:34
  144.2 9.7 %convolution_bitcast_fusion = f32[3,1024,1024]{1,2,0:T(8,128)S(1)} fusion(bf16[3,1024,1024]{1,2,0:T(8,128)(2,1)} %reshape.287, bf16[1024,1024]{1,0:T(8,128)(2,1)} %param.19), kind=kOutput, calls=%fused_computation.97 | convolution fusion | flops 6442450944 | bytes 20971520 | tf_op jit(solution)/shard_map/td,jdc->jtc/dot_general | solution.py:194
  153.8 4.6 copy-done.9
  165.2 84.3 %while.28 = (s32[]{:T(128)}, bf16[8,1024,2,64]{1,3,2,0:T(8,128)(2,1)}, f32[8,2,1024,1]{2,1,3,0:T(2,128)}, bf16[8,1024,2,64]{1,3,2,0:T(8,128)(2,1)}, bf16[8,1024,...) while((s32[]{:T(128)}, ...), condition=%wide.region_3.4_spmd.clone, body=%wide.region_0.3_spmd.clone.sunk | while | flops 563214336 | bytes 30480980 | solution.py:203
  171.4 4.4 fusion.167
  181.9 4.4 fusion.167
  192.4 4.4 fusion.167
  202.9 4.4 fusion.167
  213.5 4.4 fusion.167
  224.0 4.4 fusion.167
  234.5 4.4 fusion.167
  245.0 4.4 fusion.167
  249.6 6.3 fusion.116
  258.7 11.5 %copy.96 = bf16[2,8,512,512]{3,1,2,0:T(8,128)(2,1)} copy(bf16[2,8,512,512]{3,2,1,0:T(8,128)(2,1)} %bitcast.274) | data formatting | bytes 16777216 | tf_op jit(solution)/shard_map/reshape | solution.py:29
  270.2 12.4 %copy.122 = bf16[128,8,8,512]{3,1,2,0:T(8,128)(2,1)} copy(bf16[128,8,8,512]{3,2,1,0:T(8,128)(2,1)} %bitcast.265) | data formatting | bytes 16777216
  282.6 14.9 %copy.97 = bf16[2,8,512,512]{2,1,3,0:T(8,128)(2,1)} copy(bf16[2,8,512,512]{3,2,1,0:T(8,128)(2,1)} %bitcast.275) | data formatting | bytes 16777216 | tf_op jit(solution)/shard_map/reshape | solution.py:29
  297.5 12.2 %copy.123 = bf16[128,8,8,512]{3,1,2,0:T(8,128)(2,1)} copy(bf16[128,8,8,512]{3,2,1,0:T(8,128)(2,1)} %bitcast.266) | data formatting | bytes 16777216
  309.7 47.8 %fusion.60 = (bf16[1024,4096]{1,0:T(8,128)(2,1)}, f32[1024,4096]{1,0:T(8,128)}) fusion(f32[4096]{0:T(1024)S(1)} %bitcast.298, bf16[1024,4096]{1,0:T(8,128)(2,1)} %bitcast.276, bf16[1024,1024]{0,1:T(8,128)(2,1)S(1)} %fusion.108.clone.4), kind=kOutput, calls=%fused_computation.67 | convolution fusion | flops 8866758656 | bytes 35667968 | tf_op jit(solution)/shard_map/dot_general | solution.py:216
  357.6 11.7 %fusion.117 = (f32[1024]{0:T(1024)S(1)}, f32[1024,1024]{0,1:T(8,128)S(1)}) fusion(f32[1024]{0:T(1024)S(1)} %copy-done.35, bf16[1024,4096]{1,0:T(8,128)(2,1)} %get-tuple-element.274, bf16[4096,1024]{0,1:T(8,128)(2,1)S(1)} %bitcast.279, f32[1024]{0:T(1024)S(1)} %copy-done.30, f32[1024]{0:T(1024)S(1)} %copy-done.26, f32[1024]{0:T(1024)S(1)} %copy-done.24, ...), kind=kOutput, calls=%fused_computation.175 | convolution fusion | flops 8597273600 | bytes 25190400 | tf_op jit(solution)/shard_map/dot_general | solution.py:219
  374.8 12.9 %convolution_convert_fusion = bf16[4096,1024]{1,0:T(8,128)(2,1)} fusion(bf16[1024,4096]{1,0:T(8,128)(2,1)S(1)} %copy-done.36, bf16[1024,1024]{0,1:T(8,128)(2,1)S(1)} %copy-done.7, f32[1024,1024]{0,1:T(8,128)S(1)} %get-tuple-element.277, f32[1024]{0:T(1024)S(1)} %broadcast_multiply_fusion.2, f32[1024]{0:T(1024)S(1)} %broadcast_multiply_fusion.3, ...), kind=kOutput, calls=%fused_computation.88 | convolution fusion | flops 8603566080 | bytes 23089152 | tf_op jit(solution)/shard_map/dot_general | solution.py:227
  387.7 14.5 %reshape.301 = bf16[8,512,2,512]{3,2,1,0:T(2,128)(2,1)} reshape(bf16[4096,1024]{1,0:T(8,128)(2,1)} %convolution_convert_fusion) | data formatting | bytes 16777216 | tf_op jit(solution)/shard_map/reshape | solution.py:70
  402.1 8.3 copy.109
  410.6 22.8 %fusion.118 = (f32[4096]{0:T(1024)}, bf16[1024,4096]{1,0:T(8,128)(2,1)S(1)}) fusion(f32[1024,4096]{1,0:T(8,128)} %get-tuple-element.275, f32[4096]{0:T(1024)S(1)} %bitcast.299, bf16[4096,1024]{0,1:T(8,128)(2,1)} %bitcast.278, f32[1024]{0:T(1024)S(1)} %broadcast_multiply_fusion.2, f32[1024,1024]{0,1:T(8,128)} %copy-done.5, ...), kind=kOutput, calls=%fused_computation.176 | convolution fusion | flops 8649699328 | bytes 39899136 | tf_op jit(solution)/shard_map/dot_general | solution.py:231
  433.3 11.9 %convolution_convert_fusion.1 = bf16[1024,4096]{1,0:T(8,128)(2,1)} fusion(bf16[1024,4096]{1,0:T(8,128)(2,1)S(1)} %get-tuple-element.280, f32[1024,1024]{0,1:T(8,128)S(1)} %copy-done.4, f32[1024]{0:T(1024)S(1)} %copy-done.30, f32[1024]{0:T(1024)S(1)} %copy-done.26, f32[1024]{0:T(1024)S(1)} %copy-done.24, f32[1024]{0:T(1024)S(1)} %copy-done.21), kind=kOutput, calls=%fused_computation.89 | convolution fusion | flops 8599371776 | bytes 20987904 | tf_op jit(solution)/shard_map/dot_general | solution.py:239
  445.3 12.2 %copy.127 = bf16[128,8,8,512]{3,2,1,0:T(8,128)(2,1)} copy(bf16[128,8,8,512]{3,1,2,0:T(8,128)(2,1)} %bitcast.280) | data formatting | bytes 16777216
  457.4 9.7 %copy.108 = bf16[2,512,8,512]{3,1,2,0:T(8,128)(2,1)} copy(bf16[2,512,8,512]{3,2,1,0:T(8,128)(2,1)} %bitcast.267) | data formatting | bytes 16777216 | tf_op jit(solution)/shard_map/reshape | solution.py:63
  467.1 17.2 %multiply_reduce_fusion.1 = (f32[1024]{0:T(1024)S(1)}, f32[1024]{0:T(1024)S(1)}, f32[1024]{0:T(1024)S(1)}, f32[1024]{0:T(1024)S(1)}, f32[1024,1024]{0,1:T(8,128)S(1)}) fusion(f32[1024,1024]{0,1:T(8,128)S(1)} %copy-done.4, f32[1024]{0:T(1024)S(1)} %copy-done.24, f32[1024]{0:T(1024)S(1)} %copy-done.21, f32[1024]{0:T(1024)S(1)} %copy-done.26, ...), kind=kOutput, calls=%fused_computation.107 | convolution fusion | flops 8608804864 | bytes 31506432 | tf_op jit(solution)/shard_map/dot_general | solution.py:243
  490.5 164.5 %while.29 = (s32[]{:T(128)}, f32[8,1024,2,64]{1,3,2,0:T(8,128)}, bf16[8,1024,2,64]{1,3,2,0:T(8,128)(2,1)}, f32[8,1024,2,64]{1,3,2,0:T(8,128)}, bf16[8,1024,2,64]...) while((s32[]{:T(128)}, f32[8,1024,2,64]{1,3,2,0:T(8,128)}, ...), condition=%wide.region_14.15_spmd.clone, body=%wide.region_12.14_spmd.clone.sunk | while | flops 1374943232 | bytes 70583408 | solution.py:259
  494.3 4.2 multiply_reduce_fusion.7
  506.9 4.3 fusion.179
  527.4 4.3 fusion.179
  535.5 4.2 multiply_reduce_fusion.7
  548.1 4.3 fusion.179
  568.6 4.3 fusion.179
  589.2 4.3 fusion.179
  609.7 4.3 fusion.179
  617.7 4.2 multiply_reduce_fusion.7
  630.2 4.3 fusion.179
  650.7 4.3 fusion.179
  660.2 5.3 fusion.79
  666.4 6.5 convolution_convert_fusion.2
  699.4 4.5 stack.36
  703.9 6.2 copy.106
  710.1 5.9 convert_bitcast_fusion.1
  715.9 4.5 stack.35
  720.5 6.1 copy.105
  726.6 6.5 pad_maximum_fusion
  733.5 6.2 fusion.114
  745.5 6.7 fusion.119
  752.2 4.5 fusion.120
  756.7 10.0 %add_add_fusion = f32[1024,1024]{0,1:T(8,128)} fusion(f32[1024,1024]{0,1:T(8,128)} %fusion.120, f32[1024,1024]{0,1:T(8,128)} %copy-done.6, f32[1024,1024]{0,1:T(8,128)} %fusion.119, bf16[1024,1024]{0,1:T(8,128)(2,1)S(1)} %bitcast.272, bf16[1024,1024]{0,1:T(8,128)(2,1)} %bitcast.285), kind=kOutput, calls=%fused_computation.108 | convolution fusion | flops 2150629376 | bytes 20971520 | tf_op jit(solution)/shard_map/dot_general | solution.py:281
  766.7 5.5 copy.111
  778.4 6.2 reduce-scatter.7.cloned.1.call-done
  784.7 5.8 all_gather.61
  791.3 81.4 %reduce-scatter.5.cloned.1.call-done = bf16[1,3,512,128]{3,2,1,0:T(8,128)(2,1)} async-done(((bf16[16,3,512,128]{3,2,1,0:T(8,128)(2,1)}), bf16[1,3,512,128]{3,2,1,0:T(8,128)(2,1)}) %reduce-scatter.5.cloned.1.call-update) | async-done | bytes 393232 | tf_op jit(solution)/shard_map/reduce_scatter | solution.py:49
  872.7 14.1 %all_gather.58 = bf16[2,3,512,128]{3,2,1,0:T(8,128)(2,1)S(1)} all-gather(bf16[1,3,512,128]{3,2,1,0:T(8,128)(2,1)} %reduce-scatter.5.cloned.1.call-done), channel_id=1, replica_groups=mesh['replica'=2,'shard'=2,'tensor'=8] {'replica'}, dimensions={0}, use_global_device_ids=true | all-gather | bytes 1179648 | tf_op jit(solution)/shard_map/all_gather | solution.py:20
  888.0 7.2 all-gather.16.cloned.1.call-done
  898.0 19.7 %all-gather.14.cloned.1.call-done = bf16[2,512,512]{2,1,0:T(8,128)(2,1)} async-done(((bf16[1,512,512]{2,1,0:T(8,128)(2,1)}), bf16[2,512,512]{2,1,0:T(8,128)(2,1)}) %all-gather.14.cloned.1.call-update) | async-done | bytes 1048592 | tf_op jit(solution)/shard_map/all_gather | solution.py:20
  (254 shorter events, 249.2 us)
Async XLA Ops:
  7.2 36.1 %copy-start = (s32[8,1024]{1,0:T(8,128)S(1)}, s32[8,1024]{1,0:T(8,128)}, u32[]{:S(2)}) copy-start(s32[8,1024]{1,0:T(8,128)} %param.20) | copy-start | bytes 98308
  7.2 20.8 %copy-start.32 = (f32[512]{0:T(512)S(1)}, f32[512]{0:T(512)}, u32[]{:S(2)}) copy-start(f32[512]{0:T(512)} %param.28) | copy-start | bytes 6148
  7.2 33.5 %copy-start.13 = (bf16[1024,1024]{1,0:T(8,128)(2,1)S(1)}, bf16[1024,1024]{1,0:T(8,128)(2,1)}, u32[]{:S(2)}) copy-start(bf16[1024,1024]{1,0:T(8,128)(2,1)} %param.33) | copy-start | bytes 6291460
  7.2 47.3 %all-gather.20.cloned.1.call-start = ((), (), s32[]{:S(2)}) async-start(), calls=%async_computation.11 | async-start | bytes 2228224 | tf_op jit(solution)/shard_map/all_gather | solution.py:28
  8.0 109.1 %all-gather.18.cloned.1.call-start = ((), (), s32[]{:S(2)}) async-start(), calls=%async_computation.10 | async-start | bytes 6684672 | tf_op jit(solution)/shard_map/all_gather | solution.py:28
  8.7 250.0 %all-gather.22.cloned.1.call-start = ((), (), s32[]{:S(2)}) async-start(), calls=%async_computation.12 | async-start | bytes 8912896 | tf_op jit(solution)/shard_map/all_gather | solution.py:28
  9.4 273.1 %all-gather.24.cloned.1.call-start = ((), (), s32[]{:S(2)}) async-start(), calls=%async_computation.13 | async-start | bytes 8912896 | tf_op jit(solution)/shard_map/all_gather | solution.py:28
  10.0 735.4 %reduce-scatter.11.cloned.1.call-start = ((), (), s32[]{:S(2)}) async-start(), calls=%async_computation.8 | async-start | bytes 8912896 | tf_op jit(solution)/shard_map/reduce_scatter | solution.py:49
  153.8 4.6 copy-start.9
  165.2 84.4 %copy-start.34 = (f32[1024]{0:T(1024)S(1)}, f32[1024]{0:T(1024)}, u32[]{:S(2)}) copy-start(f32[1024]{0:T(1024)} %param.24) | copy-start | bytes 12292
  249.6 6.4 copy-start.8
  249.6 6.4 copy-start.18
  256.0 2.0 copy-start.2
  256.0 2.0 copy-start.25
  256.0 2.0 copy-start.29
  256.0 2.6 copy-start.20
  258.0 12.2 %copy-start.23 = (f32[1024]{0:T(1024)}, f32[1024]{0:T(1024)S(1)}, u32[]{:S(2)}) copy-start(f32[1024]{0:T(1024)S(1)} %add_rsqrt_fusion.1) | copy-start | bytes 12292
  309.6 47.9 %copy-start.3 = (f32[1024,1024]{0,1:T(8,128)S(1)}, f32[1024,1024]{0,1:T(8,128)}, u32[]{:S(2)}) copy-start(f32[1024,1024]{0,1:T(8,128)} %copy-done.2) | copy-start | bytes 12582916
  309.6 47.9 %copy-start.10 = (bf16[128,8,8,512]{3,1,2,0:T(8,128)(2,1)S(1)}, bf16[128,8,8,512]{3,1,2,0:T(8,128)(2,1)}, u32[]{:S(2)}) copy-start(bf16[128,8,8,512]{3,1,2,0:T(8,128)(2,1)} %copy.123) | copy-start | bytes 25165828
  309.6 47.9 %copy-start.21 = (f32[1024]{0:T(1024)S(1)}, f32[1024]{0:T(1024)}, u32[]{:S(2)}) copy-start(f32[1024]{0:T(1024)} %copy-done.20) | copy-start | bytes 12292
  309.6 47.9 %copy-start.24 = (f32[1024]{0:T(1024)S(1)}, f32[1024]{0:T(1024)}, u32[]{:S(2)}) copy-start(f32[1024]{0:T(1024)} %copy-done.23) | copy-start | bytes 12292
  309.6 47.9 %copy-start.26 = (f32[1024]{0:T(1024)S(1)}, f32[1024]{0:T(1024)}, u32[]{:S(2)}) copy-start(f32[1024]{0:T(1024)} %param.25) | copy-start | bytes 12292
  309.7 47.9 %copy-start.30 = (f32[1024]{0:T(1024)S(1)}, f32[1024]{0:T(1024)}, u32[]{:S(2)}) copy-start(f32[1024]{0:T(1024)} %param.26) | copy-start | bytes 12292
  309.7 47.9 %copy-start.35 = (f32[1024]{0:T(1024)S(1)}, f32[1024]{0:T(1024)}, u32[]{:S(2)}) copy-start(f32[1024]{0:T(1024)} %param.30) | copy-start | bytes 12292
  369.2 4.2 copy-start.5
  369.2 3.1 copy-start.7
  369.2 3.1 copy-start.28
  369.3 5.5 copy-start.36
  410.5 346.2 %reduce-scatter.9.cloned.1.call-start = ((), (), s32[]{:S(2)}) async-start(), calls=%async_computation.6 | async-start | bytes 8912896 | tf_op jit(solution)/shard_map/reduce_scatter | solution.py:49
  410.5 22.8 %copy-start.4 = (f32[1024,1024]{0,1:T(8,128)S(1)}, f32[1024,1024]{0,1:T(8,128)}, u32[]{:S(2)}) copy-start(f32[1024,1024]{0,1:T(8,128)} %copy-done.2) | copy-start | bytes 12582916
  433.3 11.9 %copy-start.37 = (bf16[1024,4096]{1,0:T(8,128)(2,1)}, bf16[1024,4096]{1,0:T(8,128)(2,1)S(1)}, u32[]{:S(2)}) copy-start(bf16[1024,4096]{1,0:T(8,128)(2,1)S(1)} %get-tuple-element.280) | copy-start | bytes 25165828
  484.4 1.7 copy-start.16
  485.8 4.0 copy-start.6
  489.8 0.7 copy-start.19
  489.8 284.9 %all-gather.26.cloned.1.call-start = ((), (), s32[]{:S(2)}) async-start(), calls=%async_computation.14 | async-start | bytes 1622016 | tf_op jit(solution)/shard_map/all_gather | solution.py:295
  655.0 5.1 copy-start.27
  655.0 5.2 copy-start.31
  665.5 0.6 copy-start.22
  666.1 118.5 %reduce-scatter.7.cloned.1.call-start = ((), (), s32[]{:S(2)}) async-start(), calls=%async_computation.5 | async-start | bytes 2228224 | tf_op jit(solution)/shard_map/reduce_scatter | solution.py:49
  678.0 4.1 copy-start.14
  678.0 194.6 %reduce-scatter.5.cloned.1.call-start = ((), (), s32[]{:S(2)}) async-start(), calls=%async_computation.4 | async-start | bytes 6684672 | tf_op jit(solution)/shard_map/reduce_scatter | solution.py:49
  680.8 1.3 copy-start.12
  692.8 2.9 copy-start.15
  733.2 162.1 %all-gather.16.cloned.1.call-start = ((), (), s32[]{:S(2)}) async-start(), calls=%async_computation.9 | async-start | bytes 1572864 | tf_op jit(solution)/shard_map/all_gather | solution.py:20
  745.4 172.3 %all-gather.14.cloned.1.call-start = ((), (), s32[]{:S(2)}) async-start(), calls=%async_computation.7 | async-start | bytes 1572864 | tf_op jit(solution)/shard_map/all_gather | solution.py:20
  745.4 6.8 copy-start.17
  745.5 6.8 copy-start.33
  766.7 5.5 copy-start.11
  872.7 47.8 %copy-start.1 = (s32[8,1024]{1,0:T(8,128)S(1)}, s32[8,1024]{1,0:T(8,128)}, u32[]{:S(2)}) copy-start(s32[8,1024]{1,0:T(8,128)} %param.20) | copy-start | bytes 98308
Sparse Core Ops, SparseCore 0:
  10.2 44.2 all-gather.19
  56.9 60.1 all-gather.17
  119.2 73.0 all-gather.21
  194.4 72.8 all-gather.23
  410.6 102.0 reduce-scatter.10
  516.6 103.1 reduce-scatter.8
  666.3 53.8 all-gather.25
  723.9 60.7 reduce-scatter.6
  788.6 84.0 reduce-scatter.4
  874.1 21.1 all-gather.15
  896.8 20.8 all-gather.13
